TPU v7x, 256 devices: a whole 4x4x8 slice. The times are simulated.
256 devices in a mesh: kx: 8 (over z), ht: 8 (over y, core), real: 4 (over x).
Axes of the slice: x: 4, y: 4, z: 8, core: 2. Of those that a mesh axis runs over, the one named last changes fastest.
Arguments:
- velocity: float32 [3, 4, 32, 512, 128], P(None, 'real', 'kx', 'ht'), may hold values from -6 to 6
- low_index: int32 [8], replicated, may hold values from 0 to 31, as said below
- neighbours: int32 [32, 8], P('kx'), may hold values from 0 to 31, as said below
- owner_map: int32 [64], replicated, may hold values from 0 to 63, each once
- mode_counts: int32 [32], P('kx'), may hold values from 16 to 64
- helmholtz: float32 [64, 512, 512], P(('kx', 'ht')), may hold values from -0.25 to 0.25
Outputs:
- velocity_next: float32 [3, 4, 32, 512, 128], P(None, 'real', 'kx', 'ht')
Inputs may be any that keep to these rules, and one draw needn't show every extreme that they name: `low_index`: distinct values. neighbours[m, j] lies within 4 modes of m, counting circularly over the 32 modes; offsets of + 4 and - 4 both occur.
All inputs are finite; a program needn't handle non-finite values.
Results may differ from a plain program's by a relative error of at most 0.0001.
Values sent between devices are 32-bit elements; how exact they have to be, the bound alone decides.
A program may use at most 64 MiB of HBM per device.

v0:
```python
import jax
import jax.numpy as jnp
from jax import lax
from jax.sharding import PartitionSpec as P

dt_step = 0.1


def extended_2(block, sides, width):
    for axis, dim in sides:
        count = lax.axis_size(axis)
        forward = [(i, i + 1) for i in range(count - 1)]
        forward.append((count - 1, 0))
        backward = [(target, source) for source, target in forward]
        low = lax.ppermute(
            lax.slice_in_dim(block, block.shape[dim] - width, None, axis=dim), axis, forward
        )
        high = lax.ppermute(lax.slice_in_dim(block, 0, width, axis=dim), axis, backward)
        block = jnp.concatenate([low, block, high], axis=dim)
    return block


def spanwise_tables(mode_count, point_count):
    column_ids = jnp.arange(2 * mode_count)
    wavenumber = (column_ids // 2).astype(jnp.float32)
    imag_part = column_ids % 2
    positions = 2.0 * jnp.pi * jnp.arange(point_count).astype(jnp.float32) / point_count
    phases = wavenumber[:, None] * positions[None, :]
    forward = jnp.where(imag_part[:, None] == 0, jnp.cos(phases), -jnp.sin(phases)) / jnp.sqrt(
        jnp.float32(mode_count)
    )
    backward = forward.T * (2.0 * mode_count / point_count)
    return (forward, backward)


def apply_inverse(block, helmholtz, kx_count, ht_count, slots_dev, rows_ht):
    components, reals_dev, band_modes = (block.shape[0], block.shape[1], block.shape[2])
    regrouped = block.reshape(
        components, reals_dev, band_modes, kx_count, ht_count, slots_dev, 2, rows_ht
    )
    regrouped = regrouped.transpose(0, 1, 3, 2, 5, 6, 4, 7)
    regrouped = regrouped.reshape(
        components, reals_dev, kx_count * band_modes, slots_dev, 2, ht_count * rows_ht
    )
    solved = jnp.einsum("syx,crmspx->crmspy", helmholtz, regrouped, precision=lax.Precision.HIGHEST)
    solved = solved.reshape(
        components, reals_dev, kx_count, band_modes, slots_dev, 2, ht_count, rows_ht
    )
    solved = solved.transpose(0, 1, 3, 2, 6, 4, 5, 7)
    return solved.reshape(block.shape)


def local(velocity, low_index, neighbours, owner_map, mode_counts, helmholtz):
    highest = lax.Precision.HIGHEST
    components, reals_dev, band_modes, rows_ht, columns = velocity.shape
    kz_modes = columns // 2
    forward, backward = spanwise_tables(kz_modes, 4 * kz_modes)
    kx_count = lax.axis_size("kx")
    ht_count = lax.axis_size("ht")
    kx_total = band_modes * kx_count
    realizations = reals_dev * lax.axis_size("real")
    owners = kx_count * ht_count
    slots_dev = kz_modes // owners
    width_out = slots_dev * 2 * rows_ht
    low_members = low_index.shape[0]
    band_start = lax.axis_index("kx") * band_modes
    global_modes = band_start + jnp.arange(band_modes, dtype=jnp.int32)
    low_select = (low_index[:, None] == global_modes[None, :]).astype(jnp.float32)
    high_mask = 1.0 - jnp.sum(low_select, axis=0)
    offsets = (neighbours - global_modes[:, None] + kx_total // 2) % kx_total - kx_total // 2
    local_partner = jnp.arange(band_modes, dtype=jnp.int32)[:, None] + band_modes + offsets
    column_mask = ((jnp.arange(columns) // 2)[None, :] < mode_counts[:, None]).astype(jnp.float32)
    inverse_map = (
        jnp.zeros((kz_modes,), jnp.int32).at[owner_map].set(jnp.arange(kz_modes, dtype=jnp.int32))
    )
    current = velocity
    physical = jnp.dot(current, forward, precision=highest)
    extended = extended_2(physical, (("kx", 2),), band_modes)
    own_low = jnp.einsum("jm,crmyz->crjyz", low_select, physical, precision=highest)
    low_fields = lax.psum(own_low, "kx")
    high_low = jnp.zeros_like(physical)
    stresses = []
    for member in range(low_members):
        partner = jnp.take(extended, local_partner[:, member], axis=2)
        low_one = low_fields[:, :, member : member + 1]
        high_low = high_low + low_one * partner[1:2] + partner * low_one[1:2]
        weighted = physical * (partner[1:2] * high_mask[None, None, :, None, None])
        stresses.append(jnp.sum(weighted, axis=(1, 2)))
    stress = jnp.stack(stresses, axis=1)
    nonlinear = jnp.dot(high_low, backward, precision=highest)
    summed = lax.psum(stress, ("kx", "real"))
    low_forcing = jnp.dot(summed / realizations, backward, precision=highest)
    forcing = nonlinear * high_mask[None, None, :, None, None]
    forcing = (
        forcing + jnp.einsum("jm,cjyk->cmyk", low_select, low_forcing, precision=highest)[:, None]
    )
    forcing = forcing * column_mask[None, None, :, None, :]
    updated = current + dt_step * forcing
    slotted = jnp.take(
        updated.reshape(components, reals_dev, band_modes, rows_ht, kz_modes, 2), owner_map, axis=4
    )
    outgoing = slotted.reshape(components, reals_dev, band_modes, rows_ht, owners, slots_dev, 2)
    outgoing = outgoing.transpose(0, 1, 2, 4, 5, 6, 3)
    flat_out = outgoing.reshape(components, reals_dev, band_modes, owners, width_out)
    applied = apply_inverse(
        lax.all_to_all(flat_out, ("kx", "ht"), split_axis=3, concat_axis=3, tiled=True),
        helmholtz,
        kx_count,
        ht_count,
        slots_dev,
        rows_ht,
    )
    returned = lax.all_to_all(applied, ("kx", "ht"), split_axis=3, concat_axis=3, tiled=True)
    restored = returned.reshape(components, reals_dev, band_modes, owners, slots_dev, 2, rows_ht)
    restored = restored.transpose(0, 1, 2, 6, 3, 4, 5).reshape(
        components, reals_dev, band_modes, rows_ht, kz_modes, 2
    )
    current = jnp.take(restored, inverse_map, axis=4).reshape(
        components, reals_dev, band_modes, rows_ht, columns
    )
    return current


def solution(mesh):
    in_specs = (
        P(None, "real", "kx", "ht", None),
        P(),
        P("kx", None),
        P(),
        P("kx"),
        P(("kx", "ht"), None, None),
    )
    out_specs = P(None, "real", "kx", "ht", None)
    return jax.shard_map(local, mesh=mesh, in_specs=in_specs, out_specs=out_specs, check_vma=False)
```

profile of v0, /device:TPU:1, one launch (start us, length us, event | category | flops | bytes accessed | tf_op | source)
XLA Modules:
  0.0 327.1 jit_solution(15920989410416831472)
XLA Ops:
  6.6 2.4 fusion.12
  9.0 2.5 collective-permute-start
  11.5 4.0 %collective-permute-start.1 = (f32[3,1,4,64,256]{4,3,2,0,1:T(8,128)S(1)}, f32[3,1,4,64,256]{4,3,2,0,1:T(8,128)}, u32[]{:S(2)}, u32[]{:S(2)}) collective-permute-start(f32[3,1,4,64,256]{4,3,2,0,1:T(8,128)S(1)} %bitcast.259), channel_id=1, source_target_pairs={{32,0},{64,32},{96,64},{128,96},{160,128},{192,160},{224,192},{0,2... | collective-permute-start | bytes 2359304 | tf_op jit(solution)/shard_map/ppermute | solution.py:18
  15.6 3.1 convolution_bitcast_fusion
  18.9 0.3 slice_reduce_fusion.7
  19.8 12.9 %collective-permute-done = f32[3,1,4,64,256]{4,3,2,0,1:T(8,128)S(1)} collective-permute-done((f32[3,1,4,64,256]{4,3,2,0,1:T(8,128)S(1)}, f32[3,1,4,64,256]{4,3,2,0,1:T(8,128)S(1)}, u32[]{:S(2)}, u32[]{:S(2)}) %collective-permute-start) | collective-permute-done | bytes 786464 | tf_op jit(solution)/shard_map/ppermute | solution.py:15
  32.7 0.9 copy-done.16
  33.6 1.8 maximum_bitcast_fusion
  35.4 1.6 gather_fusion.7
  37.0 1.5 gather_fusion.5
  38.5 1.5 gather_fusion.4
  40.0 1.5 gather_fusion.3
  41.5 1.5 gather_fusion.2
  43.0 1.5 gather_fusion.1
  44.5 1.5 gather_fusion
  46.0 1.5 gather_fusion.6
  47.5 1.4 bitcast_select_fusion.2
  48.9 1.3 bitcast_select_fusion.4
  50.8 0.6 copy-done.10
  52.1 1.4 multiply_bitcast_fusion.1
  53.7 0.5 multiply_reduce_fusion
  55.4 3.9 %stack.35 = f32[3,8,64,256]{3,1,2,0:T(8,128)} concatenate(f32[3,1,64,256]{3,1,2,0:T(1,128)S(1)} %stack.27, f32[3,1,64,256]{3,1,2,0:T(1,128)S(1)} %stack.28, f32[3,1,64,256]{3,1,2,0:T(1,128)S(1)} %stack.29, f32[3,1,64,256]{3,1,2,0:T(1,128)S(1)} %stack.30, f32[3,1,64,256]{3,1,2,0:T(1,128)S(1)} %stack.31, f32[3,1,64,256]{3,1,2,0:T(1,128)S(1)} %stack.32, ...), dimensions={1} | concatenate | bytes 3145728 | tf_op jit(solution)/shard_map/stack | solution.py:89
  59.3 0.5 copy-done.31
  59.8 0.5 compare_and_fusion.1
  60.4 35.1 %all-reduce.3.cloned.1.call-done = f32[3,1,8,64,256]{4,2,3,0,1:T(8,128)} async-done(((f32[3,1,8,64,256]{4,2,3,0,1:T(8,128)}), f32[3,1,8,64,256]{4,2,3,0,1:T(8,128)}) %all-reduce.3.cloned.1.call-update) | async-done | bytes 1572880 | tf_op jit(solution)/shard_map/psum | solution.py:80
  95.5 7.7 %fusion.51 = (f32[3,1,1,64,256]{4,2,3,0,1:T(1,128)S(1)}, f32[3,1,1,64,256]{4,2,3,0,1:T(1,128)S(1)}, f32[3,1,1,64,256]{4,2,3,0,1:T(1,128)S(1)}, f32[3,1,1,64,256]...) fusion(f32[3,1,8,64,256]{4,2,3,0,1:T(8,128)} %all-reduce.3.clon, ...), kind=kLoop, calls=%fused_computation.172 | loop fusion | bytes 3145728 | tf_op jit(solution)/shard_map/slice | solution.py:85
  103.2 0.7 copy.102
  103.8 0.7 copy.103
  104.5 0.7 copy.104
  105.2 0.7 copy.105
  105.9 0.7 copy.106
  106.6 0.7 copy.107
  107.3 0.7 copy.108
  108.0 0.7 copy.109
  108.7 3.5 %fusion.52 = (f32[1,1,1,64,256]{4,2,3,0,1:T(1,128)S(1)}, f32[1,1,1,64,256]{4,2,3,0,1:T(1,128)S(1)}, f32[1,1,1,64,256]{4,2,3,0,1:T(1,128)S(1)}, f32[1,1,1,64,256]...) fusion(f32[3,1,8,64,256]{4,2,3,0,1:T(8,128)} %all-reduce.3.clon, ...), kind=kLoop, calls=%fused_computation.173 | loop fusion | bytes 1048576 | tf_op jit(solution)/shard_map/slice | solution.py:86
  112.2 0.6 copy.112
  112.8 0.6 copy.113
  113.5 0.6 copy.114
  114.1 0.6 copy.115
  114.7 0.6 copy.116
  115.3 0.6 copy.117
  116.0 133.7 %all-reduce.5.cloned.1.call-done = f32[3,8,64,256]{3,1,2,0:T(8,128)} async-done(((f32[3,8,64,256]{3,1,2,0:T(8,128)}), f32[3,8,64,256]{3,1,2,0:T(8,128)}) %all-reduce.5.cloned.1.call-update) | async-done | bytes 1572880 | tf_op jit(solution)/shard_map/psum | solution.py:91
  249.7 3.5 %fusion = f32[3,8,64,128]{3,1,2,0:T(8,128)S(1)} fusion(f32[3,8,64,256]{3,1,2,0:T(8,128)} %all-reduce.5.cloned.1.call-done, f32[256]{0:T(256)S(1)} %convert_multiply_fusion, f32[128]{0:T(128)} %copy-done.17, pred[128]{0:T(512)(128)(4,1)S(1)} %fusion.42), kind=kOutput, calls=%fused_computation.12 | convolution fusion | flops 604504064 | bytes 2360960 | tf_op jit(solution)/shard_map/dot_general | solution.py:92
  253.2 1.2 fusion.50
  254.4 5.9 %fusion.6 = f32[3,1,4,64,128]{4,3,2,0,1:T(8,128)} fusion(f32[3,1,4,64,128]{4,3,2,1,0:T(8,128)S(1)} %copy-done.14, f32[3,64,128,4]{2,3,1,0:T(4,128)S(1)} %fusion.50, f32[4,128]{1,0:T(4,128)S(1)} %compare_convert_fusion.1, f32[4]{0:T(128)} %copy-done.27, f32[256]{0:T(256)S(1)} %convert_multiply_fusion, f32[128]{0:T(128)} %copy-done.17, ...), kind=kOutput, calls=%fused_computation.21 | convolution fusion | flops 310280192 | bytes 11669168 | tf_op jit(solution)/shard_map/dot_general | solution.py:90
  260.3 1.3 copy.38
  261.6 0.5 copy.101
  262.1 1.0 gather_fusion.8
  263.2 0.2 fusion.7
  263.4 0.4 copy.55
  263.8 0.6 reshape.457
  264.4 27.5 %all_to_all.10 = f32[3,1,4,64,128]{4,2,0,1,3:T(4,128)S(1)} all-to-all(f32[3,1,4,64,128]{4,2,0,1,3:T(4,128)S(1)} %reshape.457), channel_id=1, replica_groups=mesh['kx'=8,'ht'=8,'real'=4] {'kx','ht'}, dimensions={3} | all-to-all | bytes 786432 | tf_op jit(solution)/shard_map/all_to_all | solution.py:106
  292.0 0.5 reshape.287
  292.8 1.5 convolution_bitcast_fusion.1
  294.3 0.6 copy.56
  294.9 1.3 reshape.459
  296.2 5.5 %all-to-all-start.1 = ((f32[3,1,4,64,128]{4,2,0,1,3:T(4,128)}), f32[3,1,4,64,128]{4,2,0,1,3:T(4,128)S(1)}, u32[]{:S(2)}, u32[]{:S(2)}) async-start(f32[3,1,4,64,128]{4,2,0,1,3:T(4,128)} %reshape.459), calls=%async_computation.1 | async-start | bytes 786432 | tf_op jit(solution)/shard_map/all_to_all | solution.py:113
  301.6 0.9 scatter_custom_fusion
  302.6 14.2 %all-to-all-done.1 = f32[3,1,4,64,128]{4,2,0,1,3:T(4,128)S(1)} async-done(((f32[3,1,4,64,128]{4,2,0,1,3:T(4,128)}), f32[3,1,4,64,128]{4,2,0,1,3:T(4,128)S(1)}, u32[]{:S(2)}, u32[]{:S(2)}) %all-to-all-start.1) | async-done | bytes 393248 | tf_op jit(solution)/shard_map/all_to_all | solution.py:113
  316.8 0.5 reshape.460
  317.5 1.1 gather_fusion.9
  318.6 0.2 bitcast_select_fusion
  318.8 0.4 copy.48
  319.3 1.0 copy.49
  (129 shorter events, 3.6 us)
Async XLA Ops:
  6.5 286.2 %copy-start = (f32[1,512,512]{2,1,0:T(8,128)S(1)}, f32[1,512,512]{2,1,0:T(8,128)}, u32[]{:S(2)}) copy-start(f32[1,512,512]{2,1,0:T(8,128)} %param.15) | copy-start | bytes 3145732
  6.5 89.0 %all-reduce.3.cloned.1.call-start = ((), (), s32[]{:S(2)}) async-start(), calls=%async_computation.2 | async-start | bytes 3145728 | tf_op jit(solution)/shard_map/psum | solution.py:80
  6.6 12.2 %copy-start.17 = (f32[128]{0:T(128)}, f32[128]{0:T(128)S(1)}, u32[]{:S(2)}) copy-start(f32[128]{0:T(128)S(1)} %fusion.45) | copy-start | bytes 1540
  6.6 12.2 %copy-start.28 = (s32[4,8]{1,0:T(4,128)S(1)}, s32[4,8]{1,0:T(4,128)}, u32[]{:S(2)}) copy-start(s32[4,8]{1,0:T(4,128)} %param.12) | copy-start | bytes 388
  6.6 13.0 %copy-start.29 = (s32[8]{0:T(128)S(1)}, s32[8]{0:T(128)}, u32[]{:S(2)}) copy-start(s32[8]{0:T(128)} %param.11) | copy-start | bytes 100
  9.0 23.7 %copy-start.1 = (f32[256,3,4,64]{0,3,2,1:T(8,128)}, f32[256,3,4,64]{0,3,2,1:T(8,128)S(1)}, u32[]{:S(2)}) copy-start(f32[256,3,4,64]{0,3,2,1:T(8,128)S(1)} %fusion.12) | copy-start | bytes 2359300
  9.0 23.7 %collective-permute-start = (f32[3,1,4,64,256]{4,3,2,0,1:T(8,128)S(1)}, f32[3,1,4,64,256]{4,3,2,0,1:T(8,128)S(1)}, u32[]{:S(2)}, u32[]{:S(2)}) collective-permute-start(f32[3,1,4,64,256]{4,3,2,0,1:T(8,128)S(1)} %bitcast.258), channel_id=1, source_target_pairs={{0,32},{32,64},{64,96},{96,128},{128,160},{160,192},{192,224},{224... | collective-permute-start | bytes 2359304 | tf_op jit(solution)/shard_map/ppermute | solution.py:15
  11.5 22.1 %collective-permute-start.1 = (f32[3,1,4,64,256]{4,3,2,0,1:T(8,128)S(1)}, f32[3,1,4,64,256]{4,3,2,0,1:T(8,128)}, u32[]{:S(2)}, u32[]{:S(2)}) collective-permute-start(f32[3,1,4,64,256]{4,3,2,0,1:T(8,128)S(1)} %bitcast.259), channel_id=1, source_target_pairs={{32,0},{64,32},{96,64},{128,96},{160,128},{192,160},{224,192},{0,2... | collective-permute-start | bytes 2359304 | tf_op jit(solution)/shard_map/ppermute | solution.py:18
  15.6 19.9 %copy-start.18 = (s32[4]{0:T(128)}, s32[4]{0:T(128)S(1)}, u32[]{:S(2)}) copy-start(s32[4]{0:T(128)S(1)} %get-tuple-element.70) | copy-start | bytes 52
  18.8 230.9 %all-reduce.5.cloned.1.call-start = ((), (), s32[]{:S(2)}) async-start(), calls=%async_computation.3 | async-start | bytes 3145728 | tf_op jit(solution)/shard_map/psum | solution.py:91
  19.2 28.2 %copy-start.19 = (pred[4]{0:T(512)(128)(4,1)}, pred[4]{0:T(512)(128)(4,1)S(1)}, u32[]{:S(2)}) copy-start(pred[4]{0:T(512)(128)(4,1)S(1)} %compare_and_fusion.2) | copy-start | bytes 16
  19.3 29.6 %copy-start.20 = (pred[4]{0:T(512)(128)(4,1)}, pred[4]{0:T(512)(128)(4,1)S(1)}, u32[]{:S(2)}) copy-start(pred[4]{0:T(512)(128)(4,1)S(1)} %compare_and_fusion.4) | copy-start | bytes 16
  19.3 30.9 %copy-start.21 = (pred[4]{0:T(512)(128)(4,1)}, pred[4]{0:T(512)(128)(4,1)S(1)}, u32[]{:S(2)}) copy-start(pred[4]{0:T(512)(128)(4,1)S(1)} %compare_and_fusion.5) | copy-start | bytes 16
  19.3 31.1 %copy-start.22 = (pred[4]{0:T(512)(128)(4,1)}, pred[4]{0:T(512)(128)(4,1)S(1)}, u32[]{:S(2)}) copy-start(pred[4]{0:T(512)(128)(4,1)S(1)} %compare_and_fusion.6) | copy-start | bytes 16
  19.4 31.2 %copy-start.23 = (pred[4]{0:T(512)(128)(4,1)}, pred[4]{0:T(512)(128)(4,1)S(1)}, u32[]{:S(2)}) copy-start(pred[4]{0:T(512)(128)(4,1)S(1)} %compare_and_fusion.7) | copy-start | bytes 16
  19.4 31.4 %copy-start.24 = (pred[4]{0:T(512)(128)(4,1)}, pred[4]{0:T(512)(128)(4,1)S(1)}, u32[]{:S(2)}) copy-start(pred[4]{0:T(512)(128)(4,1)S(1)} %compare_and_fusion.8) | copy-start | bytes 16
  19.7 31.8 %copy-start.25 = (pred[4]{0:T(512)(128)(4,1)}, pred[4]{0:T(512)(128)(4,1)S(1)}, u32[]{:S(2)}) copy-start(pred[4]{0:T(512)(128)(4,1)S(1)} %compare_and_fusion.9) | copy-start | bytes 16
  19.8 32.1 %copy-start.26 = (pred[4]{0:T(512)(128)(4,1)}, pred[4]{0:T(512)(128)(4,1)S(1)}, u32[]{:S(2)}) copy-start(pred[4]{0:T(512)(128)(4,1)S(1)} %compare_and_fusion.3) | copy-start | bytes 16
  19.8 32.3 %copy-start.27 = (f32[4]{0:T(128)}, f32[4]{0:T(128)S(1)}, u32[]{:S(2)}) copy-start(f32[4]{0:T(128)S(1)} %broadcast_subtract_fusion) | copy-start | bytes 52
  32.7 0.9 copy-start.16
  47.5 2.8 copy-start.5
  47.5 3.0 copy-start.6
  48.9 1.7 copy-start.8
  50.3 1.2 copy-start.10
  50.4 1.2 copy-start.12
  50.6 1.4 copy-start.13
  52.1 1.6 copy-start.2
  55.3 3.9 %copy-start.33 = (s32[64]{0:T(128)S(1)}, s32[64]{0:T(128)}, u32[]{:S(2)}) copy-start(s32[64]{0:T(128)} %param.13) | copy-start | bytes 772
  55.4 5.0 %copy-start.32 = (s32[4]{0:T(128)S(1)}, s32[4]{0:T(128)}, u32[]{:S(2)}) copy-start(s32[4]{0:T(128)} %param.14) | copy-start | bytes 52
  59.3 0.5 copy-start.31
  112.2 142.2 %copy-start.3 = (f32[4,3,64,256]{3,2,1,0:T(8,128)S(1)}, f32[4,3,64,256]{3,2,1,0:T(8,128)}, u32[]{:S(2)}) copy-start(f32[4,3,64,256]{3,2,1,0:T(8,128)} %gather_fusion.7) | copy-start | bytes 2359300
  112.2 142.2 %copy-start.4 = (f32[4,3,64,256]{3,2,1,0:T(8,128)S(1)}, f32[4,3,64,256]{3,2,1,0:T(8,128)}, u32[]{:S(2)}) copy-start(f32[4,3,64,256]{3,2,1,0:T(8,128)} %gather_fusion.5) | copy-start | bytes 2359300
  249.7 4.7 %copy-start.7 = (f32[4,3,64,256]{3,2,1,0:T(8,128)S(1)}, f32[4,3,64,256]{3,2,1,0:T(8,128)}, u32[]{:S(2)}) copy-start(f32[4,3,64,256]{3,2,1,0:T(8,128)} %gather_fusion.3) | copy-start | bytes 2359300
  249.7 4.7 %copy-start.9 = (f32[4,3,64,256]{3,2,1,0:T(8,128)S(1)}, f32[4,3,64,256]{3,2,1,0:T(8,128)}, u32[]{:S(2)}) copy-start(f32[4,3,64,256]{3,2,1,0:T(8,128)} %gather_fusion.2) | copy-start | bytes 2359300
  249.7 4.7 %copy-start.11 = (f32[4,3,64,256]{3,2,1,0:T(8,128)S(1)}, f32[4,3,64,256]{3,2,1,0:T(8,128)}, u32[]{:S(2)}) copy-start(f32[4,3,64,256]{3,2,1,0:T(8,128)} %gather_fusion.1) | copy-start | bytes 2359300
  249.7 4.7 %copy-start.14 = (f32[3,1,4,64,128]{4,3,2,1,0:T(8,128)S(1)}, f32[3,1,4,64,128]{4,3,2,1,0:T(8,128)}, u32[]{:S(2)}) copy-start(f32[3,1,4,64,128]{4,3,2,1,0:T(8,128)} %param.10) | copy-start | bytes 1179652
  249.7 4.7 %copy-start.15 = (f32[4,64,256]{2,1,0:T(8,128)S(1)}, f32[4,64,256]{2,1,0:T(8,128)}, u32[]{:S(2)}) copy-start(f32[4,64,256]{2,1,0:T(8,128)} %get-tuple-element.40) | copy-start | bytes 786436
  262.1 1.1 copy-start.30
  296.2 20.6 %all-to-all-start.1 = ((f32[3,1,4,64,128]{4,2,0,1,3:T(4,128)}), f32[3,1,4,64,128]{4,2,0,1,3:T(4,128)S(1)}, u32[]{:S(2)}, u32[]{:S(2)}) async-start(f32[3,1,4,64,128]{4,2,0,1,3:T(4,128)} %reshape.459), calls=%async_computation.1 | async-start | bytes 786432 | tf_op jit(solution)/shard_map/all_to_all | solution.py:113
Sparse Core Ops, SparseCore 0:
  18.9 76.5 all-reduce.2
  98.9 150.7 all-reduce.4
where the time goes:
time: 328 us; the launch traced here: 327 us
  waiting for transfers between devices  196 us (60%)
  local copies, waits for them, and re-layouts  50.8 us (15%)
  blocking collectives  27.5 us (8%)
  matrix products  17.6 us (5%)
  between operations  14.4 us (4%)
  starting transfers between devices  12.1 us (4%)
  other arithmetic  8.77 us (3%)
    psum x1, waiting for transfers between devices, local(): summed = lax.psum(stress, ('kx', 'real'))  134 us
    psum x1, waiting for transfers between devices, local(): low_fields = lax.psum(own_low, 'kx')  35.1 us
    all_to_all x1, blocking collectives, local(): lax.all_to_all(flat_out, ('kx', 'ht'), split_axis=3, concat_axis=3, tiled...  27.5 us
    all_to_all x1, waiting for transfers between devices, local(): lax.all_to_all(applied, ('kx', 'ht'), split_axis=3, concat_axis=3, tiled=...  14.2 us
    ppermute x1, waiting for transfers between devices, extended_2(): lax.ppermute(lax.slice_in_dim(block, block.shape[dim] - width, None, axis...  12.9 us
    gather x8, local copies, waits for them, and re-layouts, local(): partner = jnp.take(extended, local_partner[:, member], axis=2)  12 us
    unnamed x84, local copies, waits for them, and re-layouts  11.8 us
    slice x1, local copies, waits for them, and re-layouts, local(): low_one = low_fields[:, :, member:member + 1]  7.67 us
  transfers between devices with their start and end apart: 5, of which 4 were waited for; matrix products, arithmetic and copies ran while one was open for 15% of the time, Pallas kernels for 0%

commit v1 on v0

--- a/solution.py
+++ b/solution.py
@@ -77,7 +77,11 @@
     physical = jnp.dot(current, forward, precision=highest)
     extended = extended_2(physical, (("kx", 2),), band_modes)
     own_low = jnp.einsum("jm,crmyz->crjyz", low_select, physical, precision=highest)
-    low_fields = lax.psum(own_low, "kx")
+    low_fields = own_low
+    for hop in (1, 2, 4):
+        low_fields = low_fields + lax.ppermute(
+            low_fields, "kx", [(dev, dev ^ hop) for dev in range(8)]
+        )
     high_low = jnp.zeros_like(physical)
     stresses = []
     for member in range(low_members):

time: 328 us -> 378 us (1.15)
  waiting for transfers between devices: 196 us -> 246 us
  local copies, waits for them, and re-layouts: 50.8 us -> 31.3 us
  other arithmetic: 8.77 us -> 23.9 us
  starting transfers between devices: 12.1 us -> 21.3 us
  matrix products: 17.6 us -> 13.3 us
    ppermute x0 -> x3, waiting for transfers between devices: none -> 75 us  [local(): lax.ppermute(low_fields, 'kx', [(dev, dev ^ hop) for dev in range(8)])]
    psum x1 -> x0, waiting for transfers between devices: 35.1 us -> none  [local(): low_fields = lax.psum(own_low, 'kx')]
    psum x1, waiting for transfers between devices: 134 us -> 143 us  [local(): summed = lax.psum(stress, ('kx', 'real'))]
    ppermute x0 -> x3, starting transfers between devices: none -> 9.31 us  [local(): lax.ppermute(low_fields, 'kx', [(dev, dev ^ hop) for dev in range(8)])]
    unnamed x84 -> x70, local copies, waits for them, and re-layouts: 11.8 us -> 2.91 us
    select_n x16, other arithmetic: 3.58 us -> 11 us  [local(): partner = jnp.take(extended, local_partner[:, member], axis=2)]
    add x0 -> x3, other arithmetic: none -> 6.92 us  [local(): low_fields + lax.ppermute(low_fields, 'kx', [(dev, dev ^ hop) for dev in...]
    slice x1, local copies, waits for them, and re-layouts: 7.67 us -> 1.45 us  [local(): low_one = low_fields[:, :, member:member + 1]]
  transfers between devices with their start and end apart: 5 -> 7, of which waited for: 4 -> 5; matrix products, arithmetic and copies ran while one was open for 15% -> 12% of each run, Pallas kernels for 0% -> 0%
where the time goes in v1:
time: 378 us; the launch traced here: 377 us
  waiting for transfers between devices  246 us (65%)
  local copies, waits for them, and re-layouts  31.3 us (8%)
  blocking collectives  27.5 us (7%)
  other arithmetic  23.9 us (6%)
  starting transfers between devices  21.3 us (6%)
  between operations  14.3 us (4%)
  matrix products  13.3 us (4%)
    psum x1, waiting for transfers between devices, local(): summed = lax.psum(stress, ('kx', 'real'))  143 us
    ppermute x3, waiting for transfers between devices, local(): lax.ppermute(low_fields, 'kx', [(dev, dev ^ hop) for dev in range(8)])  75 us
    all_to_all x1, blocking collectives, local(): lax.all_to_all(flat_out, ('kx', 'ht'), split_axis=3, concat_axis=3, tiled...  27.5 us
    all_to_all x1, waiting for transfers between devices, local(): lax.all_to_all(applied, ('kx', 'ht'), split_axis=3, concat_axis=3, tiled=...  14.3 us
    ppermute x1, waiting for transfers between devices, extended_2(): lax.ppermute(lax.slice_in_dim(block, block.shape[dim] - width, None, axis...  13.1 us
    gather x8, local copies, waits for them, and re-layouts, local(): partner = jnp.take(extended, local_partner[:, member], axis=2)  12 us
    select_n x16, other arithmetic, local(): partner = jnp.take(extended, local_partner[:, member], axis=2)  11 us
    ppermute x3, starting transfers between devices, local(): lax.ppermute(low_fields, 'kx', [(dev, dev ^ hop) for dev in range(8)])  9.31 us
  transfers between devices with their start and end apart: 7, of which 5 were waited for; matrix products, arithmetic and copies ran while one was open for 12% of the time, Pallas kernels for 0%

profile of v1, /device:TPU:1, one launch (start us, length us, event | category | flops | bytes accessed | tf_op | source)
XLA Modules:
  0.0 377.1 jit_solution(3601382060062478295)
XLA Ops:
  6.6 2.4 fusion.12
  9.0 2.5 collective-permute-start.3
  11.5 4.0 %collective-permute-start.4 = (f32[3,1,4,64,256]{4,3,2,0,1:T(8,128)S(1)}, f32[3,1,4,64,256]{4,3,2,0,1:T(8,128)}, u32[]{:S(2)}, u32[]{:S(2)}) collective-permute-start(f32[3,1,4,64,256]{4,3,2,0,1:T(8,128)S(1)} %bitcast.259), channel_id=1, source_target_pairs={{32,0},{64,32},{96,64},{128,96},{160,128},{192,160},{224,192},{0,2... | collective-permute-start | bytes 2359304 | tf_op jit(solution)/shard_map/ppermute | solution.py:18
  15.6 3.1 convolution_bitcast_fusion
  18.8 0.3 slice_reduce_fusion.7
  19.6 13.1 %collective-permute-done.3 = f32[3,1,4,64,256]{4,3,2,0,1:T(8,128)S(1)} collective-permute-done((f32[3,1,4,64,256]{4,3,2,0,1:T(8,128)S(1)}, f32[3,1,4,64,256]{4,3,2,0,1:T(8,128)S(1)}, u32[]{:S(2)}, u32[]{:S(2)}) %collective-permute-start.3) | collective-permute-done | bytes 786464 | tf_op jit(solution)/shard_map/ppermute | solution.py:15
  32.7 0.9 copy-done.22
  33.6 1.8 maximum_bitcast_fusion
  35.4 1.5 gather_fusion.7
  36.9 1.6 gather_fusion.5
  38.5 1.5 gather_fusion.4
  40.0 1.5 gather_fusion.3
  41.5 1.5 gather_fusion.2
  42.9 1.5 gather_fusion.1
  44.5 1.5 gather_fusion
  46.0 2.3 bitcast_select_fusion.2
  48.2 2.2 bitcast_select_fusion.4
  50.5 1.1 bitcast_select_fusion.5
  51.5 1.1 bitcast_select_fusion.6
  52.6 1.0 bitcast_select_fusion.7
  53.6 1.0 bitcast_select_fusion.8
  54.7 9.2 %collective-permute-done = f32[3,1,8,64,256]{4,2,3,0,1:T(8,128)} collective-permute-done((f32[3,1,8,64,256]{4,2,3,0,1:T(8,128)}, f32[3,1,8,64,256]{4,2,3,0,1:T(8,128)}, u32[]{:S(2)}, u32[]{:S(2)}) %collective-permute-start) | collective-permute-done | bytes 1572896 | tf_op jit(solution)/shard_map/ppermute | solution.py:82
  63.8 3.2 add.144
  67.1 4.3 %collective-permute-start.1 = (f32[3,1,8,64,256]{4,2,3,0,1:T(8,128)}, f32[3,1,8,64,256]{4,2,3,0,1:T(8,128)}, u32[]{:S(2)}, u32[]{:S(2)}) collective-permute-start(f32[3,1,8,64,256]{4,2,3,0,1:T(8,128)} %add.144), channel_id=1, source_target_pairs={{0,64},{32,96},{64,0},{96,32},{128,192},{160,224},{192,128},{224,1... | collective-permute-start | bytes 4718600 | tf_op jit(solution)/shard_map/ppermute | solution.py:82
  71.4 1.0 bitcast_select_fusion.9
  72.4 1.5 gather_fusion.6
  73.9 1.3 bitcast_select_fusion.3
  75.2 2.7 multiply_bitcast_fusion.1
  77.9 0.5 multiply_reduce_fusion
  79.5 3.7 stack.35
  83.3 65.8 %collective-permute-done.1 = f32[3,1,8,64,256]{4,2,3,0,1:T(8,128)} collective-permute-done((f32[3,1,8,64,256]{4,2,3,0,1:T(8,128)}, f32[3,1,8,64,256]{4,2,3,0,1:T(8,128)}, u32[]{:S(2)}, u32[]{:S(2)}) %collective-permute-start.1) | collective-permute-done | bytes 1572896 | tf_op jit(solution)/shard_map/ppermute | solution.py:82
  149.1 2.1 add.145
  151.1 5.0 %collective-permute-start.2 = (f32[3,1,8,64,256]{4,2,3,0,1:T(8,128)S(1)}, f32[3,1,8,64,256]{4,2,3,0,1:T(8,128)}, u32[]{:S(2)}, u32[]{:S(2)}) collective-permute-start(f32[3,1,8,64,256]{4,2,3,0,1:T(8,128)S(1)} %add.145), channel_id=1, source_target_pairs={{0,128},{32,160},{64,192},{96,224},{128,0},{160,32},{192,64},{224,... | collective-permute-start | bytes 4718600 | tf_op jit(solution)/shard_map/ppermute | solution.py:82
  156.3 143.1 %all-reduce.2.cloned.1.call-done = f32[3,8,64,256]{3,1,2,0:T(8,128)} async-done(((f32[3,8,64,256]{3,1,2,0:T(8,128)}), f32[3,8,64,256]{3,1,2,0:T(8,128)}) %all-reduce.2.cloned.1.call-update) | async-done | bytes 1572880 | tf_op jit(solution)/shard_map/psum | solution.py:95
  299.3 3.3 fusion
  302.7 0.5 fusion.50
  303.2 1.6 add.146
  304.9 1.5 fusion.51
  306.4 0.4 fusion.52
  307.2 0.4 copy-done.12
  307.6 0.3 copy-done.3
  308.0 0.2 copy-done.4
  308.2 0.2 copy-done.6
  308.4 0.2 copy-done.8
  308.7 0.2 copy-done.10
  308.9 2.4 fusion.6
  311.4 0.3 copy.38
  311.6 0.5 copy.101
  312.2 1.0 gather_fusion.8
  313.2 0.2 fusion.7
  313.4 0.4 copy.55
  313.9 0.6 reshape.457
  314.4 27.5 %all_to_all.10 = f32[3,1,4,64,128]{4,2,0,1,3:T(4,128)S(1)} all-to-all(f32[3,1,4,64,128]{4,2,0,1,3:T(4,128)S(1)} %reshape.457), channel_id=1, replica_groups=mesh['kx'=8,'ht'=8,'real'=4] {'kx','ht'}, dimensions={3} | all-to-all | bytes 786432 | tf_op jit(solution)/shard_map/all_to_all | solution.py:110
  342.0 0.5 reshape.287
  342.8 1.5 convolution_bitcast_fusion.1
  344.3 0.6 copy.56
  344.9 1.3 reshape.459
  346.2 5.4 %all-to-all-start.1 = ((f32[3,1,4,64,128]{4,2,0,1,3:T(4,128)}), f32[3,1,4,64,128]{4,2,0,1,3:T(4,128)S(1)}, u32[]{:S(2)}, u32[]{:S(2)}) async-start(f32[3,1,4,64,128]{4,2,0,1,3:T(4,128)} %reshape.459), calls=%async_computation.1 | async-start | bytes 786432 | tf_op jit(solution)/shard_map/all_to_all | solution.py:117
  351.7 0.8 scatter_custom_fusion
  352.5 14.3 %all-to-all-done.1 = f32[3,1,4,64,128]{4,2,0,1,3:T(4,128)S(1)} async-done(((f32[3,1,4,64,128]{4,2,0,1,3:T(4,128)}), f32[3,1,4,64,128]{4,2,0,1,3:T(4,128)S(1)}, u32[]{:S(2)}, u32[]{:S(2)}) %all-to-all-start.1) | async-done | bytes 393248 | tf_op jit(solution)/shard_map/all_to_all | solution.py:117
  366.8 0.5 reshape.460
  367.6 1.1 gather_fusion.9
  368.9 0.4 copy.48
  369.3 1.0 copy.49
  (121 shorter events, 2.8 us)
Async XLA Ops:
  6.5 336.3 %copy-start = (f32[1,512,512]{2,1,0:T(8,128)S(1)}, f32[1,512,512]{2,1,0:T(8,128)}, u32[]{:S(2)}) copy-start(f32[1,512,512]{2,1,0:T(8,128)} %param.15) | copy-start | bytes 3145732
  6.5 12.8 %copy-start.24 = (s32[8]{0:T(128)S(1)}, s32[8]{0:T(128)}, u32[]{:S(2)}) copy-start(s32[8]{0:T(128)} %param.11) | copy-start | bytes 100
  6.5 12.2 %copy-start.23 = (s32[4,8]{1,0:T(4,128)S(1)}, s32[4,8]{1,0:T(4,128)}, u32[]{:S(2)}) copy-start(s32[4,8]{1,0:T(4,128)} %param.12) | copy-start | bytes 388
  6.5 292.8 %all-reduce.2.cloned.1.call-start = ((), (), s32[]{:S(2)}) async-start(), calls=%async_computation.2 | async-start | bytes 3145728 | tf_op jit(solution)/shard_map/psum | solution.py:95
  9.0 23.7 %copy-start.1 = (f32[256,3,4,64]{0,3,2,1:T(8,128)}, f32[256,3,4,64]{0,3,2,1:T(8,128)S(1)}, u32[]{:S(2)}) copy-start(f32[256,3,4,64]{0,3,2,1:T(8,128)S(1)} %fusion.12) | copy-start | bytes 2359300
  9.0 23.7 %collective-permute-start.3 = (f32[3,1,4,64,256]{4,3,2,0,1:T(8,128)S(1)}, f32[3,1,4,64,256]{4,3,2,0,1:T(8,128)S(1)}, u32[]{:S(2)}, u32[]{:S(2)}) collective-permute-start(f32[3,1,4,64,256]{4,3,2,0,1:T(8,128)S(1)} %bitcast.258), channel_id=1, source_target_pairs={{0,32},{32,64},{64,96},{96,128},{128,160},{160,192},{192,224},{224... | collective-permute-start | bytes 2359304 | tf_op jit(solution)/shard_map/ppermute | solution.py:15
  11.5 22.1 %collective-permute-start.4 = (f32[3,1,4,64,256]{4,3,2,0,1:T(8,128)S(1)}, f32[3,1,4,64,256]{4,3,2,0,1:T(8,128)}, u32[]{:S(2)}, u32[]{:S(2)}) collective-permute-start(f32[3,1,4,64,256]{4,3,2,0,1:T(8,128)S(1)} %bitcast.259), channel_id=1, source_target_pairs={{32,0},{64,32},{96,64},{128,96},{160,128},{192,160},{224,192},{0,2... | collective-permute-start | bytes 2359304 | tf_op jit(solution)/shard_map/ppermute | solution.py:18
  18.7 45.1 %collective-permute-start = (f32[3,1,8,64,256]{4,2,3,0,1:T(8,128)}, f32[3,1,8,64,256]{4,2,3,0,1:T(8,128)}, u32[]{:S(2)}, u32[]{:S(2)}) collective-permute-start(f32[3,1,8,64,256]{4,2,3,0,1:T(8,128)} %convolution_bitcast_fusion), channel_id=1, source_target_pairs={{0,32},{32,0},{64,96},{96,64},{128,160},{160,128},{192,224},{224,1... | collective-permute-start | bytes 4718600 | tf_op jit(solution)/shard_map/ppermute | solution.py:82
  32.7 0.9 copy-start.22
  46.0 4.5 %copy-start.5 = (f32[4,3,64,256]{3,2,1,0:T(8,128)S(1)}, f32[4,3,64,256]{3,2,1,0:T(8,128)}, u32[]{:S(2)}) copy-start(f32[4,3,64,256]{3,2,1,0:T(8,128)} %gather_fusion.4) | copy-start | bytes 2359300
  46.0 5.6 %copy-start.7 = (f32[4,3,64,256]{3,2,1,0:T(8,128)S(1)}, f32[4,3,64,256]{3,2,1,0:T(8,128)}, u32[]{:S(2)}) copy-start(f32[4,3,64,256]{3,2,1,0:T(8,128)} %gather_fusion.3) | copy-start | bytes 2359300
  48.2 4.4 %copy-start.9 = (f32[4,3,64,256]{3,2,1,0:T(8,128)S(1)}, f32[4,3,64,256]{3,2,1,0:T(8,128)}, u32[]{:S(2)}) copy-start(f32[4,3,64,256]{3,2,1,0:T(8,128)} %gather_fusion.2) | copy-start | bytes 2359300
  50.5 3.2 copy-start.11
  54.7 16.7 %copy-start.13 = (f32[4,3,64,256]{3,2,1,0:T(8,128)S(1)}, f32[4,3,64,256]{3,2,1,0:T(8,128)}, u32[]{:S(2)}) copy-start(f32[4,3,64,256]{3,2,1,0:T(8,128)} %gather_fusion) | copy-start | bytes 2359300
  67.1 82.0 %collective-permute-start.1 = (f32[3,1,8,64,256]{4,2,3,0,1:T(8,128)}, f32[3,1,8,64,256]{4,2,3,0,1:T(8,128)}, u32[]{:S(2)}, u32[]{:S(2)}) collective-permute-start(f32[3,1,8,64,256]{4,2,3,0,1:T(8,128)} %add.144), channel_id=1, source_target_pairs={{0,64},{32,96},{64,0},{96,32},{128,192},{160,224},{192,128},{224,1... | collective-permute-start | bytes 4718600 | tf_op jit(solution)/shard_map/ppermute | solution.py:82
  75.2 2.7 copy-start.2
  83.2 72.9 %copy-start.26 = (s32[64]{0:T(128)S(1)}, s32[64]{0:T(128)}, u32[]{:S(2)}) copy-start(s32[64]{0:T(128)} %param.13) | copy-start | bytes 772
  83.2 72.9 %copy-start.25 = (s32[4]{0:T(128)S(1)}, s32[4]{0:T(128)}, u32[]{:S(2)}) copy-start(s32[4]{0:T(128)} %param.14) | copy-start | bytes 52
  151.1 152.1 %collective-permute-start.2 = (f32[3,1,8,64,256]{4,2,3,0,1:T(8,128)S(1)}, f32[3,1,8,64,256]{4,2,3,0,1:T(8,128)}, u32[]{:S(2)}, u32[]{:S(2)}) collective-permute-start(f32[3,1,8,64,256]{4,2,3,0,1:T(8,128)S(1)} %add.145), channel_id=1, source_target_pairs={{0,128},{32,160},{64,192},{96,224},{128,0},{160,32},{192,64},{224,... | collective-permute-start | bytes 4718600 | tf_op jit(solution)/shard_map/ppermute | solution.py:82
  304.8 2.3 copy-start.14
  304.8 2.3 copy-start.15
  304.8 2.3 copy-start.17
  304.9 2.3 copy-start.18
  304.9 2.3 copy-start.19
  304.9 2.3 copy-start.20
  304.9 2.3 copy-start.21
  306.4 1.2 copy-start.12
  306.4 1.3 copy-start.16
  306.7 1.2 copy-start.3
  306.8 1.4 copy-start.4
  306.8 1.7 copy-start.6
  306.8 1.9 copy-start.8
  306.8 2.1 copy-start.10
  346.2 20.6 %all-to-all-start.1 = ((f32[3,1,4,64,128]{4,2,0,1,3:T(4,128)}), f32[3,1,4,64,128]{4,2,0,1,3:T(4,128)S(1)}, u32[]{:S(2)}, u32[]{:S(2)}) async-start(f32[3,1,4,64,128]{4,2,0,1,3:T(4,128)} %reshape.459), calls=%async_computation.1 | async-start | bytes 786432 | tf_op jit(solution)/shard_map/all_to_all | solution.py:117
Sparse Core Ops, SparseCore 0:
  83.3 215.9 all-reduce.1
